TPU v7x, 32 devices: a whole 2x2x4 slice. The times are simulated.
32 devices in a mesh: groups: 2 (over x), seq: 16 (over z, y, core).
Axes of the slice: x: 2, y: 2, z: 4, core: 2. Of those that a mesh axis runs over, the one named last changes fastest.
Arguments:
- enc_input: bfloat16 [8192, 1408], P(('groups', 'seq')), parts along dimension 0, may hold values from -6 to 6
- enc_weight: bfloat16 [2816, 1536], P('seq'), may hold values from -0.109375 to 0.109375
- norm_gain: float32 [1536], replicated, may hold values from 0.5 to 1.5
- q_weight: bfloat16 [1536, 1024], replicated, may hold values from -1 to 1
- kv_weight: bfloat16 [1536, 320], replicated, may hold values from -1 to 1
- out_weight: bfloat16 [1536, 1536], replicated, may hold values from -0.15625 to 0.15625
- dec_weight: float32 [3, 1536], replicated, may hold values from -3 to 3
- track_weight: bfloat16 [192, 1536], P('seq'), may hold values from -0.15625 to 0.15625
- track_grad: bfloat16 [4096, 192], P('groups', 'seq'), parts along dimension 0, may hold values from -6 to 6
- track_index: int32 [384], P('groups'), parts along dimension 0, may hold values from 0 to 191, each once
- track_mask: int32 [384], P('groups'), parts along dimension 0, may hold values 0 or 1
Outputs:
- trunk_out: bfloat16 [4096, 1536], P(('groups', 'seq')), parts along dimension 0
- skip_grad: bfloat16 [4096, 1536], P(('groups', 'seq')), parts along dimension 0
- dec_weight_grad: float32 [6, 1536], P('groups'), parts along dimension 0
There are 2 independent parts, one for each index of `groups`. A program takes and returns all parts, laid end to end along the dimension named above; an argument that names none is the same for every part. Nothing has to cross between parts.
Inputs may be any that keep to these rules, and one draw needn't show every extreme that they name: `track_index`: names every track once.
All inputs are finite; a program needn't handle non-finite values.
Results may differ from a plain program's by a relative error of at most 0.02.
Values may be sent and summed in bfloat16 or wider, within the bound.
No kernel may reach another device: no remote copies, remote signals or barrier semaphores. Data moves between devices by JAX's collectives and lax.ppermute only.
A program may use at most 128 MiB of HBM per device.

v0:
```python
import math
import jax
import jax.numpy as jnp
from jax import lax
from jax.sharding import PartitionSpec as P

HEADS = 8
QK = 128
VDIM = 192
DILATION_SPAN = 8


def with_halo(cells, sides, width):
    for axis, dim in sides:
        count = lax.axis_size(axis)
        ends = count - 1
        head = lax.slice_in_dim(cells, 0, width, axis=dim)
        tail = lax.slice_in_dim(cells, cells.shape[dim] - width, cells.shape[dim], axis=dim)
        cells = jnp.concatenate(
            [
                lax.ppermute(tail, axis, [(i, (i + 1) % count) for i in range(ends)]),
                cells,
                lax.ppermute(head, axis, [((i + 1) % count, i) for i in range(ends)]),
            ],
            axis=dim,
        )
    return cells


def gelu_tanh(values):
    return jax.nn.gelu(values, approximate=True)


def attention(tokens, tok_f, norm_gain, q_weight, kv_weight, out_weight):
    token_rows = tokens.shape[0]
    normed = (
        tok_f * lax.rsqrt(jnp.mean(tok_f * tok_f, axis=-1, keepdims=True) + 1e-06) * norm_gain
    ).astype(jnp.bfloat16)
    query = jnp.dot(normed, q_weight, preferred_element_type=jnp.float32).astype(jnp.bfloat16)
    keyval = jnp.dot(normed, kv_weight, preferred_element_type=jnp.float32).astype(jnp.bfloat16)
    query_rows = query.reshape(token_rows * HEADS, QK)

    def block_update(carry, key_block):
        running_max, running_sum, weighted = carry
        scores = lax.dot_general(
            query_rows,
            key_block[:, :QK],
            (((1,), (1,)), ((), ())),
            preferred_element_type=jnp.float32,
        ) * QK ** (-0.5)
        new_max = jnp.maximum(running_max, jnp.max(scores, axis=1))
        shrink = jnp.exp(running_max - new_max)
        expw = jnp.exp(scores - new_max[:, None])
        running_sum = running_sum * shrink + jnp.sum(expw, axis=1)
        weighted = weighted * shrink[:, None] + jnp.dot(
            expw.astype(jnp.bfloat16), key_block[:, QK:], preferred_element_type=jnp.float32
        )
        return (new_max, running_sum, weighted)

    start_state = (
        jnp.full((token_rows * HEADS,), -1e30, jnp.float32),
        jnp.zeros((token_rows * HEADS,), jnp.float32),
        jnp.zeros((token_rows * HEADS, VDIM), jnp.float32),
    )
    carry = start_state
    piece = lax.all_gather(keyval, "seq", axis=0, tiled=True)
    count = piece.shape[0]

    def step_fn(inner, key_block):
        return (block_update(inner, key_block), 0)

    carry, unused = lax.scan(step_fn, carry, piece.reshape(count // 128, 128, piece.shape[1]))
    running_max, running_sum, weighted = carry
    context = (
        (weighted / running_sum[:, None]).reshape(token_rows, HEADS * VDIM).astype(jnp.bfloat16)
    )
    return (tok_f + jnp.dot(context, out_weight, preferred_element_type=jnp.float32)).astype(
        jnp.bfloat16
    )


def decoder_back(tok_f, dec_weight, track_weight, track_grad, track_index, track_mask):
    token_rows = tok_f.shape[0]
    exchanged = lax.all_to_all(track_grad, "seq", split_axis=0, concat_axis=1, tiled=True)
    masked = exchanged * track_mask.astype(jnp.bfloat16)[None, :]
    every_row = lax.all_gather(track_weight, "seq", axis=0, tiled=True)
    selected = jnp.take(every_row, track_index, axis=0)
    head_f = jnp.dot(masked, selected, preferred_element_type=jnp.float32)
    head_gradient = head_f.astype(jnp.bfloat16)
    padded_input = with_halo(head_gradient, (("seq", 0),), DILATION_SPAN).astype(jnp.float32)
    skip_act, pullback = jax.vjp(gelu_tanh, tok_f)
    convback = jnp.zeros(tok_f.shape, jnp.float32)
    tap_terms = []
    for shift_amount in range(3):
        shifted_rows = padded_input[
            DILATION_SPAN * (2 - shift_amount) : DILATION_SPAN * (2 - shift_amount) + token_rows
        ]
        convback = convback + dec_weight[shift_amount][None, :] * shifted_rows
        tap_terms.append(jnp.sum(skip_act * shifted_rows, axis=0))
    skip_grad = pullback(convback)[0].astype(jnp.bfloat16)
    summed = lax.psum(jnp.stack(tap_terms, axis=0), "seq")
    dec_weight_grad = summed / jnp.float32(math.sqrt(token_rows * lax.axis_size("seq")))
    return (skip_grad, dec_weight_grad)


def shards(
    enc_input,
    enc_weight,
    norm_gain,
    q_weight,
    kv_weight,
    out_weight,
    dec_weight,
    track_weight,
    track_grad,
    track_index,
    track_mask,
):
    token_rows = enc_input.shape[0] // 2
    patches = enc_input.reshape(token_rows, 2 * enc_input.shape[1])
    tok_sum = jnp.dot(
        patches,
        lax.all_gather(enc_weight, "seq", axis=0, tiled=True),
        preferred_element_type=jnp.float32,
    )
    tokens = tok_sum.astype(jnp.bfloat16)
    tok_f = tokens.astype(jnp.float32)
    trunk_out = attention(tokens, tok_f, norm_gain, q_weight, kv_weight, out_weight)
    skip_grad, dec_weight_grad = decoder_back(
        tok_f, dec_weight, track_weight, track_grad, track_index, track_mask
    )
    return (trunk_out, skip_grad, dec_weight_grad)


def solution(mesh):
    return jax.shard_map(
        shards,
        mesh=mesh,
        in_specs=(
            P(("groups", "seq"), None),
            P("seq", None),
            P(),
            P(),
            P(),
            P(),
            P(),
            P("seq", None),
            P("groups", "seq"),
            P("groups"),
            P("groups"),
        ),
        out_specs=(P(("groups", "seq"), None), P(("groups", "seq"), None), P("groups", None)),
        check_vma=False,
    )
```

profile of v0, /device:TPU:0, one launch (start us, length us, event | category | flops | bytes accessed | tf_op | source)
XLA Modules:
  0.0 272.7 jit_solution(8789962556055584525)
XLA Ops:
  9.6 7.4 %all-to-all-start = ((bf16[16,128,12]{1,2,0:T(8,128)(2,1)}), bf16[16,128,12]{1,2,0:T(8,128)(2,1)S(1)}, u32[]{:S(2)}, u32[]{:S(2)}) async-start(bf16[16,128,12]{1,2,0:T(8,128)(2,1)} %copy.20), calls=%async_computation | async-start | bytes 131072 | tf_op jit(solution)/shard_map/all_to_all | solution.py:84
  17.1 30.1 %all-gather = bf16[16,12,1536]{2,1,0:T(8,128)(2,1)} all-gather(bf16[1,12,1536]{2,1,0:T(8,128)(2,1)} %bitcast.28), channel_id=1, replica_groups=mesh['groups'=2,'seq'=16] {'seq'}, dimensions={0}, use_global_device_ids=true | all-gather | bytes 626688 | tf_op jit(solution)/shard_map/all_gather | solution.py:86
  51.3 3.6 %gather_fusion = bf16[192,1536]{1,0:T(8,128)(2,1)} fusion(bf16[192,1536]{1,0:T(8,128)(2,1)} %reshape.51, s32[1024]{0:T(1024)S(1)} %pad_clamp_fusion), kind=kCustom, calls=%fused_computation | custom fusion | bytes 1180416 | tf_op jit(solution)/shard_map/jit(_take)/gather | solution.py:87
  57.7 2.8 %collective-permute-start = (bf16[8,1536]{1,0:T(8,128)(2,1)}, bf16[8,1536]{1,0:T(8,128)(2,1)}, u32[]{:S(2)}, u32[]{:S(2)}) collective-permute-start(bf16[8,1536]{1,0:T(8,128)(2,1)} %get-tuple-element.101), channel_id=1, source_target_pairs={{0,1},{1,2},{2,3},{3,4},{4,5},{5,6},{6,7},{7,8},{8,9},{9,10},{10,1... | collective-permute-start | bytes 73736 | tf_op jit(solution)/shard_map/ppermute | solution.py:21
  67.2 26.1 %all-gather.4.cloned.1.call-done = bf16[2816,1536]{1,0:T(8,128)(2,1)} async-done(((bf16[176,1536]{1,0:T(8,128)(2,1)}), bf16[2816,1536]{1,0:T(8,128)(2,1)}) %all-gather.4.cloned.1.call-update) | async-done | bytes 8650768 | tf_op jit(solution)/shard_map/all_gather | solution.py:123
  93.3 7.5 %multiply_reduce_fusion.3 = (f32[1536]{0:T(1024)S(1)}, f32[1536]{0:T(1024)S(1)}, f32[1536]{0:T(1024)S(1)}, f32[128]{0:T(128)S(1)}, bf16[128,1536]{1,0:T(8,128)(2,1)}, /*index=5*/f32[128,1536]{1,0:T(8,128)S(1)}) fusion(f32[144,1536]{1,0:T(8,128)} %maximum_convert_fusion, f32[1536]{0:T(1024)S(1)} %get-tuple-element.82, f32[1536]{0:T(1024)} %get-tuple-element.83, ...), kind=kOutput, calls=%fused_computation.34 | convolution fusion | flops 1114172800 | bytes 12947968 | tf_op jit(solution)/shard_map/dot_general | solution.py:121
  106.4 59.2 %psum.7 = f32[3,1536]{1,0:T(4,128)S(1)} all-reduce(f32[3,1536]{1,0:T(4,128)S(1)} %pad_maximum_fusion), channel_id=1, replica_groups=mesh['groups'=2,'seq'=16] {'seq'}, use_global_device_ids=true, to_apply=%region_8.9 | all-reduce | flops 4608 | bytes 36864 | tf_op jit(solution)/shard_map/psum | solution.py:101
  166.2 2.6 copy.21
  168.7 89.4 %while.15 = (s32[]{:T(128)}, f32[1024]{0:T(1024)S(1)}, f32[1024]{0:T(1024)S(1)}, f32[1024,192]{0,1:T(8,128)}, bf16[16,128,320]{2,1,0:T(8,128)(2,1)}, /*index=5*/bf16[1024,128]{1,0:T(8,128)(2,1)S(1)}, s32[]{:T(128)}, s32[]{:T(128)}) while((s32[]{:T(128)}, f32[1024]{0:T(1024)S(1)}, f32[1024]{0:T(1024)S(1)}, f32[1024,192]{0,1:T(8,128)}, ...), condition=%wide.region_4.5_spmd.clone, body=%wide.region_1.4_spmd.clone.sunk | while | flops 85267456 | bytes 3735653 | solution.py:72
  177.2 2.5 convolution_add_fusion.3
  182.8 2.5 convolution_add_fusion.3
  188.4 2.5 convolution_add_fusion.3
  194.0 2.5 convolution_add_fusion.3
  199.6 2.5 convolution_add_fusion.3
  205.2 2.5 convolution_add_fusion.3
  210.8 2.5 convolution_add_fusion.3
  216.4 2.5 convolution_add_fusion.3
  222.0 2.5 convolution_add_fusion.3
  227.6 2.5 convolution_add_fusion.3
  233.2 2.5 convolution_add_fusion.3
  238.8 2.5 convolution_add_fusion.3
  244.4 2.5 convolution_add_fusion.3
  250.0 2.5 convolution_add_fusion.3
  261.8 4.1 %fusion.8 = bf16[128,1536]{1,0:T(8,128)(2,1)} fusion(f32[128,1536]{1,0:T(8,128)} %copy-done.1, bf16[128,1536]{1,0:T(8,128)(2,1)S(1)} %convert_element_type.46, bf16[1536,1536]{1,0:T(8,128)(2,1)} %param.18), kind=kOutput, calls=%fused_computation.19 | convolution fusion | flops 604372992 | bytes 6291456 | tf_op jit(solution)/shard_map/dot_general | solution.py:77
  (144 shorter events, 80.2 us)
Async XLA Ops:
  7.2 95.6 %copy-start = (bf16[1536,1024]{1,0:T(8,128)(2,1)S(1)}, bf16[1536,1024]{1,0:T(8,128)(2,1)}, u32[]{:S(2)}) copy-start(bf16[1536,1024]{1,0:T(8,128)(2,1)} %param.16) | copy-start | bytes 9437188
  7.2 86.1 %all-gather.4.cloned.1.call-start = ((), (), s32[]{:S(2)}) async-start(), calls=%async_computation.1 | async-start | bytes 9191424 | tf_op jit(solution)/shard_map/all_gather | solution.py:123
  9.6 45.3 %all-to-all-start = ((bf16[16,128,12]{1,2,0:T(8,128)(2,1)}), bf16[16,128,12]{1,2,0:T(8,128)(2,1)S(1)}, u32[]{:S(2)}, u32[]{:S(2)}) async-start(bf16[16,128,12]{1,2,0:T(8,128)(2,1)} %copy.20), calls=%async_computation | async-start | bytes 131072 | tf_op jit(solution)/shard_map/all_to_all | solution.py:84
  17.0 149.2 %all-gather.6.cloned.1.call-start = ((), (), s32[]{:S(2)}) async-start(), calls=%async_computation.2 | async-start | bytes 1392640 | tf_op jit(solution)/shard_map/all_gather | solution.py:66
  57.7 7.7 %collective-permute-start = (bf16[8,1536]{1,0:T(8,128)(2,1)}, bf16[8,1536]{1,0:T(8,128)(2,1)}, u32[]{:S(2)}, u32[]{:S(2)}) collective-permute-start(bf16[8,1536]{1,0:T(8,128)(2,1)} %get-tuple-element.101), channel_id=1, source_target_pairs={{0,1},{1,2},{2,3},{3,4},{4,5},{5,6},{6,7},{7,8},{8,9},{9,10},{10,1... | collective-permute-start | bytes 73736 | tf_op jit(solution)/shard_map/ppermute | solution.py:21
  60.5 4.9 %collective-permute-start.1 = (bf16[8,1536]{1,0:T(8,128)(2,1)}, bf16[8,1536]{1,0:T(8,128)(2,1)}, u32[]{:S(2)}, u32[]{:S(2)}) collective-permute-start(bf16[8,1536]{1,0:T(8,128)(2,1)} %get-tuple-element.102), channel_id=1, source_target_pairs={{1,0},{2,1},{3,2},{4,3},{5,4},{6,5},{7,6},{8,7},{9,8},{10,9},{11,1... | collective-permute-start | bytes 73736 | tf_op jit(solution)/shard_map/ppermute | solution.py:23
  93.3 8.3 %copy-start.2 = (bf16[1536,320]{0,1:T(8,128)(2,1)S(1)}, bf16[1536,320]{0,1:T(8,128)(2,1)}, u32[]{:S(2)}) copy-start(bf16[1536,320]{0,1:T(8,128)(2,1)} %param.17) | copy-start | bytes 2949124
  93.3 8.3 %copy-start.3 = (f32[1536]{0:T(1024)S(1)}, f32[1536]{0:T(1024)}, u32[]{:S(2)}) copy-start(f32[1536]{0:T(1024)} %param.15) | copy-start | bytes 18436
  100.7 0.9 copy-start.1
Sparse Core Ops, SparseCore 0:
  10.3 82.9 all-gather.3
  102.9 36.2 all-gather.5
where the time goes:
time: 275 us; the launch traced here: 273 us
  blocking collectives  89.3 us (32%)
  matrix products  72.9 us (27%)
  local copies, waits for them, and re-layouts  33.7 us (12%)
  waiting for transfers between devices  26.8 us (10%)
  other arithmetic  24.2 us (9%)
  between operations  14.2 us (5%)
  starting transfers between devices  11.6 us (4%)
    psum x1, blocking collectives, decoder_back(): summed = lax.psum(jnp.stack(tap_terms, axis=0), 'seq')  59.2 us
    dot_general x16, matrix products, block_update(): jnp.dot(expw.astype(jnp.bfloat16), key_block[:, QK:], preferred_element_t...  39.6 us
    all_gather x1, blocking collectives, decoder_back(): every_row = lax.all_gather(track_weight, 'seq', axis=0, tiled=True)  30.1 us
    all_gather x1, waiting for transfers between devices, shards(): lax.all_gather(enc_weight, 'seq', axis=0, tiled=True)  26.1 us
    reduce_sum x16, other arithmetic, block_update(): running_sum = running_sum * shrink + jnp.sum(expw, axis=1)  18.2 us
    dot_general x16, matrix products, block_update(): lax.dot_general(query_rows, key_block[:, :QK], (((1,), (1,)), ((), ())),...  16.7 us
    squeeze x16, local copies, waits for them, and re-layouts, attention(): lax.scan(step_fn, carry, piece.reshape(count // 128, 128, piece.shape[1]))  14.4 us
    dot_general x1, matrix products, shards(): jnp.dot(patches, lax.all_gather(enc_weight, 'seq', axis=0, tiled=True), p...  7.46 us
  transfers between devices with their start and end apart: 5, of which 1 were waited for; matrix products, arithmetic and copies ran while one was open for 8% of the time, Pallas kernels for 0%

commit v1 on v0

--- a/solution.py
+++ b/solution.py
@@ -83,7 +83,14 @@
     token_rows = tok_f.shape[0]
     exchanged = lax.all_to_all(track_grad, "seq", split_axis=0, concat_axis=1, tiled=True)
     masked = exchanged * track_mask.astype(jnp.bfloat16)[None, :]
-    every_row = lax.all_gather(track_weight, "seq", axis=0, tiled=True)
+    size = lax.axis_size("seq")
+    right = [(i_2, (i_2 + 1) % size) for i_2 in range(size)]
+    blocks = [track_weight]
+    for stride in range(1, size):
+        blocks = [lax.ppermute(blocks[0], "seq", right), *blocks]
+    out = jnp.concatenate(blocks, axis=0)
+    offset = (lax.axis_index("seq") + 1) * blocks[-1].shape[0]
+    every_row = jnp.roll(out, offset, axis=0)
     selected = jnp.take(every_row, track_index, axis=0)
     head_f = jnp.dot(masked, selected, preferred_element_type=jnp.float32)
     head_gradient = head_f.astype(jnp.bfloat16)

time: 275 us -> 354 us (1.29)
  waiting for transfers between devices: 26.8 us -> 92.8 us
  local copies, waits for them, and re-layouts: 33.7 us -> 74.9 us
  blocking collectives: 89.3 us -> 59.9 us
    ppermute x0 -> x15, waiting for transfers between devices: none -> 92.1 us  [decoder_back(): blocks = [lax.ppermute(blocks[0], 'seq', right), *blocks]]
    concatenate x0 -> x1, local copies, waits for them, and re-layouts: none -> 40.5 us  [decoder_back(): every_row = jnp.roll(out, offset, axis=0)]
    all_gather x1 -> x0, blocking collectives: 30.1 us -> none  [decoder_back(): every_row = lax.all_gather(track_weight, 'seq', axis=0, tiled=True)]
    all_gather x1, waiting for transfers between devices: 26.1 us -> 0.01 us  [shards(): lax.all_gather(enc_weight, 'seq', axis=0, tiled=True)]
  transfers between devices with their start and end apart: 5 -> 20, of which waited for: 1 -> 15; matrix products, arithmetic and copies ran while one was open for 8% -> 18% of each run, Pallas kernels for 0% -> 0%
where the time goes in v1:
time: 354 us; the launch traced here: 350 us
  waiting for transfers between devices  92.8 us (26%)
  local copies, waits for them, and re-layouts  74.9 us (21%)
  matrix products  72.4 us (20%)
  blocking collectives  59.9 us (17%)
  other arithmetic  25.8 us (7%)
  between operations  14.2 us (4%)
  starting transfers between devices  9.6 us (3%)
    ppermute x15, waiting for transfers between devices, decoder_back(): blocks = [lax.ppermute(blocks[0], 'seq', right), *blocks]  92.1 us
    psum x1, blocking collectives, decoder_back(): summed = lax.psum(jnp.stack(tap_terms, axis=0), 'seq')  59.9 us
    concatenate x1, local copies, waits for them, and re-layouts, decoder_back(): every_row = jnp.roll(out, offset, axis=0)  40.5 us
    dot_general x16, matrix products, block_update(): jnp.dot(expw.astype(jnp.bfloat16), key_block[:, QK:], preferred_element_t...  39.4 us
    reduce_sum x16, other arithmetic, block_update(): running_sum = running_sum * shrink + jnp.sum(expw, axis=1)  18.2 us
    dot_general x16, matrix products, block_update(): lax.dot_general(query_rows, key_block[:, :QK], (((1,), (1,)), ((), ())),...  16.4 us
    squeeze x16, local copies, waits for them, and re-layouts, attention(): lax.scan(step_fn, carry, piece.reshape(count // 128, 128, piece.shape[1]))  14.4 us
    dot_general x1, matrix products, shards(): jnp.dot(patches, lax.all_gather(enc_weight, 'seq', axis=0, tiled=True), p...  7.51 us
  transfers between devices with their start and end apart: 20, of which 15 were waited for; matrix products, arithmetic and copies ran while one was open for 18% of the time, Pallas kernels for 0%

profile of v1, /device:TPU:0, one launch (start us, length us, event | category | flops | bytes accessed | tf_op | source)
XLA Modules:
  0.0 349.8 jit_solution(9171019349919172593)
XLA Ops:
  8.4 7.0 %collective-permute-done = bf16[12,1536]{1,0:T(8,128)(2,1)S(1)} collective-permute-done((bf16[12,1536]{1,0:T(8,128)(2,1)}, bf16[12,1536]{1,0:T(8,128)(2,1)S(1)}, u32[]{:S(2)}, u32[]{:S(2)}) %collective-permute-start) | collective-permute-done | bytes 36896 | tf_op jit(solution)/shard_map/ppermute | solution.py:90
  15.4 6.2 %collective-permute-done.1 = bf16[12,1536]{1,0:T(8,128)(2,1)S(1)} collective-permute-done((bf16[12,1536]{1,0:T(8,128)(2,1)S(1)}, bf16[12,1536]{1,0:T(8,128)(2,1)S(1)}, u32[]{:S(2)}, u32[]{:S(2)}) %collective-permute-start.1) | collective-permute-done | bytes 36896 | tf_op jit(solution)/shard_map/ppermute | solution.py:90
  21.6 7.1 %collective-permute-done.2 = bf16[12,1536]{1,0:T(8,128)(2,1)S(1)} collective-permute-done((bf16[12,1536]{1,0:T(8,128)(2,1)S(1)}, bf16[12,1536]{1,0:T(8,128)(2,1)S(1)}, u32[]{:S(2)}, u32[]{:S(2)}) %collective-permute-start.2) | collective-permute-done | bytes 36896 | tf_op jit(solution)/shard_map/ppermute | solution.py:90
  28.7 7.2 %collective-permute-done.3 = bf16[12,1536]{1,0:T(8,128)(2,1)S(1)} collective-permute-done((bf16[12,1536]{1,0:T(8,128)(2,1)S(1)}, bf16[12,1536]{1,0:T(8,128)(2,1)S(1)}, u32[]{:S(2)}, u32[]{:S(2)}) %collective-permute-start.3) | collective-permute-done | bytes 36896 | tf_op jit(solution)/shard_map/ppermute | solution.py:90
  35.9 7.2 %collective-permute-done.4 = bf16[12,1536]{1,0:T(8,128)(2,1)S(1)} collective-permute-done((bf16[12,1536]{1,0:T(8,128)(2,1)S(1)}, bf16[12,1536]{1,0:T(8,128)(2,1)S(1)}, u32[]{:S(2)}, u32[]{:S(2)}) %collective-permute-start.4) | collective-permute-done | bytes 36896 | tf_op jit(solution)/shard_map/ppermute | solution.py:90
  43.2 6.2 %collective-permute-done.5 = bf16[12,1536]{1,0:T(8,128)(2,1)S(1)} collective-permute-done((bf16[12,1536]{1,0:T(8,128)(2,1)S(1)}, bf16[12,1536]{1,0:T(8,128)(2,1)S(1)}, u32[]{:S(2)}, u32[]{:S(2)}) %collective-permute-start.5) | collective-permute-done | bytes 36896 | tf_op jit(solution)/shard_map/ppermute | solution.py:90
  49.4 7.1 %collective-permute-done.6 = bf16[12,1536]{1,0:T(8,128)(2,1)S(1)} collective-permute-done((bf16[12,1536]{1,0:T(8,128)(2,1)S(1)}, bf16[12,1536]{1,0:T(8,128)(2,1)S(1)}, u32[]{:S(2)}, u32[]{:S(2)}) %collective-permute-start.6) | collective-permute-done | bytes 36896 | tf_op jit(solution)/shard_map/ppermute | solution.py:90
  56.5 7.2 %collective-permute-done.7 = bf16[12,1536]{1,0:T(8,128)(2,1)S(1)} collective-permute-done((bf16[12,1536]{1,0:T(8,128)(2,1)S(1)}, bf16[12,1536]{1,0:T(8,128)(2,1)S(1)}, u32[]{:S(2)}, u32[]{:S(2)}) %collective-permute-start.7) | collective-permute-done | bytes 36896 | tf_op jit(solution)/shard_map/ppermute | solution.py:90
  63.8 7.2 %collective-permute-done.8 = bf16[12,1536]{1,0:T(8,128)(2,1)S(1)} collective-permute-done((bf16[12,1536]{1,0:T(8,128)(2,1)S(1)}, bf16[12,1536]{1,0:T(8,128)(2,1)S(1)}, u32[]{:S(2)}, u32[]{:S(2)}) %collective-permute-start.8) | collective-permute-done | bytes 36896 | tf_op jit(solution)/shard_map/ppermute | solution.py:90
  71.0 7.2 %collective-permute-done.9 = bf16[12,1536]{1,0:T(8,128)(2,1)S(1)} collective-permute-done((bf16[12,1536]{1,0:T(8,128)(2,1)S(1)}, bf16[12,1536]{1,0:T(8,128)(2,1)S(1)}, u32[]{:S(2)}, u32[]{:S(2)}) %collective-permute-start.9) | collective-permute-done | bytes 36896 | tf_op jit(solution)/shard_map/ppermute | solution.py:90
  79.1 6.5 %collective-permute-done.10 = bf16[12,1536]{1,0:T(8,128)(2,1)} collective-permute-done((bf16[12,1536]{1,0:T(8,128)(2,1)S(1)}, bf16[12,1536]{1,0:T(8,128)(2,1)}, u32[]{:S(2)}, u32[]{:S(2)}) %collective-permute-start.10) | collective-permute-done | bytes 36896 | tf_op jit(solution)/shard_map/ppermute | solution.py:90
  86.3 5.8 %all-to-all-start = ((bf16[16,128,12]{1,2,0:T(8,128)(2,1)}), bf16[16,128,12]{1,2,0:T(8,128)(2,1)S(1)}, u32[]{:S(2)}, u32[]{:S(2)}) async-start(bf16[16,128,12]{1,2,0:T(8,128)(2,1)} %copy.17), calls=%async_computation | async-start | bytes 131072 | tf_op jit(solution)/shard_map/all_to_all | solution.py:84
  93.4 6.1 %collective-permute-done.12 = bf16[12,1536]{1,0:T(8,128)(2,1)S(1)} collective-permute-done((bf16[12,1536]{1,0:T(8,128)(2,1)}, bf16[12,1536]{1,0:T(8,128)(2,1)S(1)}, u32[]{:S(2)}, u32[]{:S(2)}) %collective-permute-start.12) | collective-permute-done | bytes 36896 | tf_op jit(solution)/shard_map/ppermute | solution.py:90
  101.4 5.0 %collective-permute-done.13 = bf16[12,1536]{1,0:T(8,128)(2,1)} collective-permute-done((bf16[12,1536]{1,0:T(8,128)(2,1)S(1)}, bf16[12,1536]{1,0:T(8,128)(2,1)}, u32[]{:S(2)}, u32[]{:S(2)}) %collective-permute-start.13) | collective-permute-done | bytes 36896 | tf_op jit(solution)/shard_map/ppermute | solution.py:90
  108.9 4.1 %collective-permute-done.14 = bf16[12,1536]{1,0:T(8,128)(2,1)} collective-permute-done((bf16[12,1536]{1,0:T(8,128)(2,1)}, bf16[12,1536]{1,0:T(8,128)(2,1)}, u32[]{:S(2)}, u32[]{:S(2)}) %collective-permute-start.14) | collective-permute-done | bytes 36896 | tf_op jit(solution)/shard_map/ppermute | solution.py:90
  113.0 40.5 %concatenate.9 = bf16[384,1536]{1,0:T(8,128)(2,1)} concatenate(bf16[12,1536]{1,0:T(8,128)(2,1)} %collective-permute-done.14, bf16[12,1536]{1,0:T(8,128)(2,1)} %collective-permute-done.13, bf16[12,1536]{1,0:T(8,128)(2,1)} %copy-done.6, bf16[12,1536]{1,0:T(8,128)(2,1)} %collective-permute-done.11, bf16[12,1536]{1,0:T(8,128)(2,1)} %collective-permute-done.10, ...), dimensions={0} | concatenate | bytes 2359296 | tf_op jit(solution)/shard_map/jit(_roll_dynamic)/concatenate | solution.py:93
  155.5 3.8 %gather_fusion = bf16[192,1536]{1,0:T(8,128)(2,1)} fusion(bf16[192,1536]{1,0:T(8,128)(2,1)} %constant_dynamic-slice_fusion, s32[1024]{0:T(1024)} %pad_clamp_fusion), kind=kCustom, calls=%fused_computation | custom fusion | bytes 1180416 | tf_op jit(solution)/shard_map/jit(_take)/gather | solution.py:94
  170.0 7.5 %multiply_reduce_fusion.3 = (f32[1536]{0:T(1024)S(1)}, f32[1536]{0:T(1024)S(1)}, f32[1536]{0:T(1024)S(1)}, f32[128]{0:T(128)S(1)}, bf16[128,1536]{1,0:T(8,128)(2,1)}, /*index=5*/f32[128,1536]{1,0:T(8,128)S(1)}) fusion(f32[144,1536]{1,0:T(8,128)} %maximum_convert_fusion, f32[1536]{0:T(1024)S(1)} %get-tuple-element.76, f32[1536]{0:T(1024)} %get-tuple-element.77, ...), kind=kOutput, calls=%fused_computation.34 | convolution fusion | flops 1114172800 | bytes 12947968 | tf_op jit(solution)/shard_map/dot_general | solution.py:128
  183.2 59.9 %psum.7 = f32[3,1536]{1,0:T(4,128)S(1)} all-reduce(f32[3,1536]{1,0:T(4,128)S(1)} %pad_maximum_fusion), channel_id=1, replica_groups=mesh['groups'=2,'seq'=16] {'seq'}, use_global_device_ids=true, to_apply=%region_8.9 | all-reduce | flops 4608 | bytes 36864 | tf_op jit(solution)/shard_map/psum | solution.py:108
  243.8 2.6 copy.18
  246.4 88.8 %while.15 = (s32[]{:T(128)}, f32[1024]{0:T(1024)S(1)}, f32[1024]{0:T(1024)S(1)}, f32[1024,192]{0,1:T(8,128)}, bf16[16,128,320]{2,1,0:T(8,128)(2,1)}, /*index=5*/bf16[1024,128]{1,0:T(8,128)(2,1)S(1)}, s32[]{:T(128)}, s32[]{:T(128)}) while((s32[]{:T(128)}, f32[1024]{0:T(1024)S(1)}, f32[1024]{0:T(1024)S(1)}, f32[1024,192]{0,1:T(8,128)}, ...), condition=%wide.region_4.5_spmd.clone, body=%wide.region_1.4_spmd.clone.sunk | while | flops 85267456 | bytes 3735653 | solution.py:72
  277.0 2.5 convolution_add_fusion.3
  304.9 2.5 convolution_add_fusion.3
  338.9 4.1 %fusion.8 = bf16[128,1536]{1,0:T(8,128)(2,1)} fusion(f32[128,1536]{1,0:T(8,128)} %copy-done.1, bf16[128,1536]{1,0:T(8,128)(2,1)S(1)} %convert_element_type.46, bf16[1536,1536]{1,0:T(8,128)(2,1)} %param.18), kind=kOutput, calls=%fused_computation.19 | convolution fusion | flops 604372992 | bytes 6291456 | tf_op jit(solution)/shard_map/dot_general | solution.py:77
  (186 shorter events, 114.8 us)
Async XLA Ops:
  7.2 172.5 %copy-start = (bf16[1536,1024]{1,0:T(8,128)(2,1)S(1)}, bf16[1536,1024]{1,0:T(8,128)(2,1)}, u32[]{:S(2)}) copy-start(bf16[1536,1024]{1,0:T(8,128)(2,1)} %param.16) | copy-start | bytes 9437188
  7.2 162.8 %all-gather.3.cloned.1.call-start = ((), (), s32[]{:S(2)}) async-start(), calls=%async_computation.1 | async-start | bytes 9191424 | tf_op jit(solution)/shard_map/all_gather | solution.py:130
  7.9 7.5 %collective-permute-start = (bf16[12,1536]{1,0:T(8,128)(2,1)}, bf16[12,1536]{1,0:T(8,128)(2,1)S(1)}, u32[]{:S(2)}, u32[]{:S(2)}) collective-permute-start(bf16[12,1536]{1,0:T(8,128)(2,1)} %param.20), channel_id=1, source_target_pairs={{0,1},{1,2},{2,3},{3,4},{4,5},{5,6},{6,7},{7,8},{8,9},{9,10},{10,1... | collective-permute-start | bytes 110600 | tf_op jit(solution)/shard_map/ppermute | solution.py:90
  15.4 6.2 %collective-permute-start.1 = (bf16[12,1536]{1,0:T(8,128)(2,1)S(1)}, bf16[12,1536]{1,0:T(8,128)(2,1)S(1)}, u32[]{:S(2)}, u32[]{:S(2)}) collective-permute-start(bf16[12,1536]{1,0:T(8,128)(2,1)S(1)} %collective-permute-done), channel_id=1, source_target_pairs={{0,1},{1,2},{2,3},{3,4},{4,5},{5,6},{6,7},{7,8},{8,9},{9,10},{10,1... | collective-permute-start | bytes 110600 | tf_op jit(solution)/shard_map/ppermute | solution.py:90
  21.6 7.1 %collective-permute-start.2 = (bf16[12,1536]{1,0:T(8,128)(2,1)S(1)}, bf16[12,1536]{1,0:T(8,128)(2,1)S(1)}, u32[]{:S(2)}, u32[]{:S(2)}) collective-permute-start(bf16[12,1536]{1,0:T(8,128)(2,1)S(1)} %collective-permute-done.1), channel_id=1, source_target_pairs={{0,1},{1,2},{2,3},{3,4},{4,5},{5,6},{6,7},{7,8},{8,9},{9,10},{10,1... | collective-permute-start | bytes 110600 | tf_op jit(solution)/shard_map/ppermute | solution.py:90
  28.7 7.2 %collective-permute-start.3 = (bf16[12,1536]{1,0:T(8,128)(2,1)S(1)}, bf16[12,1536]{1,0:T(8,128)(2,1)S(1)}, u32[]{:S(2)}, u32[]{:S(2)}) collective-permute-start(bf16[12,1536]{1,0:T(8,128)(2,1)S(1)} %collective-permute-done.2), channel_id=1, source_target_pairs={{0,1},{1,2},{2,3},{3,4},{4,5},{5,6},{6,7},{7,8},{8,9},{9,10},{10,1... | collective-permute-start | bytes 110600 | tf_op jit(solution)/shard_map/ppermute | solution.py:90
  35.9 7.2 %collective-permute-start.4 = (bf16[12,1536]{1,0:T(8,128)(2,1)S(1)}, bf16[12,1536]{1,0:T(8,128)(2,1)S(1)}, u32[]{:S(2)}, u32[]{:S(2)}) collective-permute-start(bf16[12,1536]{1,0:T(8,128)(2,1)S(1)} %collective-permute-done.3), channel_id=1, source_target_pairs={{0,1},{1,2},{2,3},{3,4},{4,5},{5,6},{6,7},{7,8},{8,9},{9,10},{10,1... | collective-permute-start | bytes 110600 | tf_op jit(solution)/shard_map/ppermute | solution.py:90
  43.2 6.2 %collective-permute-start.5 = (bf16[12,1536]{1,0:T(8,128)(2,1)S(1)}, bf16[12,1536]{1,0:T(8,128)(2,1)S(1)}, u32[]{:S(2)}, u32[]{:S(2)}) collective-permute-start(bf16[12,1536]{1,0:T(8,128)(2,1)S(1)} %collective-permute-done.4), channel_id=1, source_target_pairs={{0,1},{1,2},{2,3},{3,4},{4,5},{5,6},{6,7},{7,8},{8,9},{9,10},{10,1... | collective-permute-start | bytes 110600 | tf_op jit(solution)/shard_map/ppermute | solution.py:90
  49.4 7.1 %collective-permute-start.6 = (bf16[12,1536]{1,0:T(8,128)(2,1)S(1)}, bf16[12,1536]{1,0:T(8,128)(2,1)S(1)}, u32[]{:S(2)}, u32[]{:S(2)}) collective-permute-start(bf16[12,1536]{1,0:T(8,128)(2,1)S(1)} %collective-permute-done.5), channel_id=1, source_target_pairs={{0,1},{1,2},{2,3},{3,4},{4,5},{5,6},{6,7},{7,8},{8,9},{9,10},{10,1... | collective-permute-start | bytes 110600 | tf_op jit(solution)/shard_map/ppermute | solution.py:90
  56.5 7.2 %collective-permute-start.7 = (bf16[12,1536]{1,0:T(8,128)(2,1)S(1)}, bf16[12,1536]{1,0:T(8,128)(2,1)S(1)}, u32[]{:S(2)}, u32[]{:S(2)}) collective-permute-start(bf16[12,1536]{1,0:T(8,128)(2,1)S(1)} %collective-permute-done.6), channel_id=1, source_target_pairs={{0,1},{1,2},{2,3},{3,4},{4,5},{5,6},{6,7},{7,8},{8,9},{9,10},{10,1... | collective-permute-start | bytes 110600 | tf_op jit(solution)/shard_map/ppermute | solution.py:90
  63.8 14.5 %copy-start.3 = (bf16[12,1536]{1,0:T(8,128)(2,1)}, bf16[12,1536]{1,0:T(8,128)(2,1)S(1)}, u32[]{:S(2)}) copy-start(bf16[12,1536]{1,0:T(8,128)(2,1)S(1)} %collective-permute-done.7) | copy-start | bytes 110596
  63.8 7.2 %collective-permute-start.8 = (bf16[12,1536]{1,0:T(8,128)(2,1)S(1)}, bf16[12,1536]{1,0:T(8,128)(2,1)S(1)}, u32[]{:S(2)}, u32[]{:S(2)}) collective-permute-start(bf16[12,1536]{1,0:T(8,128)(2,1)S(1)} %collective-permute-done.7), channel_id=1, source_target_pairs={{0,1},{1,2},{2,3},{3,4},{4,5},{5,6},{6,7},{7,8},{8,9},{9,10},{10,1... | collective-permute-start | bytes 110600 | tf_op jit(solution)/shard_map/ppermute | solution.py:90
  71.0 7.2 %collective-permute-start.9 = (bf16[12,1536]{1,0:T(8,128)(2,1)S(1)}, bf16[12,1536]{1,0:T(8,128)(2,1)S(1)}, u32[]{:S(2)}, u32[]{:S(2)}) collective-permute-start(bf16[12,1536]{1,0:T(8,128)(2,1)S(1)} %collective-permute-done.8), channel_id=1, source_target_pairs={{0,1},{1,2},{2,3},{3,4},{4,5},{5,6},{6,7},{7,8},{8,9},{9,10},{10,1... | collective-permute-start | bytes 110600 | tf_op jit(solution)/shard_map/ppermute | solution.py:90
  78.2 7.3 %collective-permute-start.10 = (bf16[12,1536]{1,0:T(8,128)(2,1)S(1)}, bf16[12,1536]{1,0:T(8,128)(2,1)}, u32[]{:S(2)}, u32[]{:S(2)}) collective-permute-start(bf16[12,1536]{1,0:T(8,128)(2,1)S(1)} %collective-permute-done.9), channel_id=1, source_target_pairs={{0,1},{1,2},{2,3},{3,4},{4,5},{5,6},{6,7},{7,8},{8,9},{9,10},{10,1... | collective-permute-start | bytes 110600 | tf_op jit(solution)/shard_map/ppermute | solution.py:90
  85.6 7.1 %collective-permute-start.11 = (bf16[12,1536]{1,0:T(8,128)(2,1)}, bf16[12,1536]{1,0:T(8,128)(2,1)}, u32[]{:S(2)}, u32[]{:S(2)}) collective-permute-start(bf16[12,1536]{1,0:T(8,128)(2,1)} %collective-permute-done.10), channel_id=1, source_target_pairs={{0,1},{1,2},{2,3},{3,4},{4,5},{5,6},{6,7},{7,8},{8,9},{9,10},{10,1... | collective-permute-start | bytes 110600 | tf_op jit(solution)/shard_map/ppermute | solution.py:90
  86.3 22.0 %all-to-all-start = ((bf16[16,128,12]{1,2,0:T(8,128)(2,1)}), bf16[16,128,12]{1,2,0:T(8,128)(2,1)S(1)}, u32[]{:S(2)}, u32[]{:S(2)}) async-start(bf16[16,128,12]{1,2,0:T(8,128)(2,1)} %copy.17), calls=%async_computation | async-start | bytes 131072 | tf_op jit(solution)/shard_map/all_to_all | solution.py:84
  92.1 151.7 %all-gather.5.cloned.1.call-start = ((), (), s32[]{:S(2)}) async-start(), calls=%async_computation.2 | async-start | bytes 1392640 | tf_op jit(solution)/shard_map/all_gather | solution.py:66
  92.7 6.8 %collective-permute-start.12 = (bf16[12,1536]{1,0:T(8,128)(2,1)}, bf16[12,1536]{1,0:T(8,128)(2,1)S(1)}, u32[]{:S(2)}, u32[]{:S(2)}) collective-permute-start(bf16[12,1536]{1,0:T(8,128)(2,1)} %collective-permute-done.11), channel_id=1, source_target_pairs={{0,1},{1,2},{2,3},{3,4},{4,5},{5,6},{6,7},{7,8},{8,9},{9,10},{10,1... | collective-permute-start | bytes 110600 | tf_op jit(solution)/shard_map/ppermute | solution.py:90
  100.1 6.3 %collective-permute-start.13 = (bf16[12,1536]{1,0:T(8,128)(2,1)S(1)}, bf16[12,1536]{1,0:T(8,128)(2,1)}, u32[]{:S(2)}, u32[]{:S(2)}) collective-permute-start(bf16[12,1536]{1,0:T(8,128)(2,1)S(1)} %collective-permute-done.12), channel_id=1, source_target_pairs={{0,1},{1,2},{2,3},{3,4},{4,5},{5,6},{6,7},{7,8},{8,9},{9,10},{10,1... | collective-permute-start | bytes 110600 | tf_op jit(solution)/shard_map/ppermute | solution.py:90
  106.4 6.5 %collective-permute-start.14 = (bf16[12,1536]{1,0:T(8,128)(2,1)}, bf16[12,1536]{1,0:T(8,128)(2,1)}, u32[]{:S(2)}, u32[]{:S(2)}) collective-permute-start(bf16[12,1536]{1,0:T(8,128)(2,1)} %collective-permute-done.13), channel_id=1, source_target_pairs={{0,1},{1,2},{2,3},{3,4},{4,5},{5,6},{6,7},{7,8},{8,9},{9,10},{10,1... | collective-permute-start | bytes 110600 | tf_op jit(solution)/shard_map/ppermute | solution.py:90
  161.4 6.8 %collective-permute-start.15 = (bf16[8,1536]{1,0:T(8,128)(2,1)}, bf16[8,1536]{1,0:T(8,128)(2,1)}, u32[]{:S(2)}, u32[]{:S(2)}) collective-permute-start(bf16[8,1536]{1,0:T(8,128)(2,1)} %get-tuple-element.95), channel_id=1, source_target_pairs={{0,1},{1,2},{2,3},{3,4},{4,5},{5,6},{6,7},{7,8},{8,9},{9,10},{10,1... | collective-permute-start | bytes 73736 | tf_op jit(solution)/shard_map/ppermute | solution.py:21
  163.3 4.9 %collective-permute-start.16 = (bf16[8,1536]{1,0:T(8,128)(2,1)}, bf16[8,1536]{1,0:T(8,128)(2,1)}, u32[]{:S(2)}, u32[]{:S(2)}) collective-permute-start(bf16[8,1536]{1,0:T(8,128)(2,1)} %get-tuple-element.96), channel_id=1, source_target_pairs={{1,0},{2,1},{3,2},{4,3},{5,4},{6,5},{7,6},{8,7},{9,8},{10,9},{11,1... | collective-permute-start | bytes 73736 | tf_op jit(solution)/shard_map/ppermute | solution.py:23
  170.0 8.4 %copy-start.2 = (bf16[1536,320]{0,1:T(8,128)(2,1)S(1)}, bf16[1536,320]{0,1:T(8,128)(2,1)}, u32[]{:S(2)}) copy-start(bf16[1536,320]{0,1:T(8,128)(2,1)} %param.17) | copy-start | bytes 2949124
  170.0 8.4 %copy-start.7 = (f32[1536]{0:T(1024)S(1)}, f32[1536]{0:T(1024)}, u32[]{:S(2)}) copy-start(f32[1536]{0:T(1024)} %param.15) | copy-start | bytes 18436
  (6 other events, 27.8 us)
Sparse Core Ops, SparseCore 0:
  10.3 82.9 all-gather.2
  179.7 37.0 all-gather.4
